TPU v7x, 512 devices: a whole 4x8x8 slice. The times are simulated.
512 devices in a mesh: ctx: 64 (over z, x, y_lo), tp: 8 (over y_hi, core).
Axes of the slice: x: 4, y: 8 (y_hi: 4, y_lo: 2; y = y_hi * 2 + y_lo), z: 8, core: 2. Of those that a mesh axis runs over, the one named last changes fastest.
Arguments:
- tokens: bfloat16 [8192, 4096], P('ctx'), may hold values from -6 to 6
- new_token_states: bfloat16 [4, 4096], replicated, may hold values from -6.0625 to 6.0625
- w_query: bfloat16 [4096, 2048], P('ctx', 'tp'), may hold values from -0.12162204 to 0.12162204
- key_matrix: bfloat16 [4096, 1024], P('ctx', 'tp'), may hold values from -0.12162204 to 0.12162204
- value_matrix: bfloat16 [4096, 1024], P('ctx', 'tp'), may hold values from -0.09375 to 0.09375
- w_out: bfloat16 [2048, 4096], P('tp', 'ctx'), may hold values from -0.125 to 0.125
- lengths: int32 [4], replicated, may hold values from 1 to 4096, 8192 in all
- block_map: int32 [128], replicated, may hold values from 0 to 127, each once
Outputs:
- prefill_out: bfloat16 [8192, 4096], P('ctx', 'tp')
- decode_out: bfloat16 [4, 4096], P(None, 'tp')
Inputs may be any that keep to these rules, and one draw needn't show every extreme that they name: The lengths sum to 8192, and some request has exactly 4096 tokens. `block_map`: each of the 128 initial blocks is held exactly once.
All inputs are finite; a program needn't handle non-finite values.
Results may differ from a plain program's by a relative error of at most 0.015.
Values may be sent and summed in bfloat16 or wider, within the bound.
A program may use at most 64 MiB of HBM per device.

v0:
```python
import math
import jax
import jax.numpy as jnp
from jax import lax
from jax.sharding import PartitionSpec as P

HEAD_SIZE = 128
floor_value = -1e30


def initial_positions(block_map, first_row, row_count, block_rows):
    row_ids = first_row + jnp.arange(row_count, dtype=jnp.int32)
    block_ids = row_ids // block_rows
    table_ids = jnp.arange(block_map.shape[0], dtype=jnp.int32)
    mapped = jnp.sum(
        jnp.where(block_ids[:, None] == table_ids[None, :], block_map[None, :], 0), axis=1
    )
    return mapped * block_rows + row_ids % block_rows


def request_index(positions, request_ends):
    return jnp.sum((positions[:, None] >= request_ends[None, :]).astype(jnp.int32), axis=1)


def round_weights(weights):
    rounded = weights.astype(jnp.bfloat16)
    rounded = lax.optimization_barrier(rounded)
    return rounded.astype(jnp.float32)


def softmax_parts(
    dec_heads, projected_key_rows, projected_value_rows, owned, kv_heads, head_dim, score_scale
):
    row_count = projected_key_rows.shape[0]
    scores = (
        jnp.einsum(
            "rgjd,tgd->rgjt",
            dec_heads,
            projected_key_rows.reshape(row_count, kv_heads, head_dim),
            preferred_element_type=jnp.float32,
        )
        * score_scale
    )
    scores = jnp.where(owned, scores, floor_value)
    part_peak = jnp.max(scores, axis=3)
    weights = jnp.where(owned, jnp.exp(scores - part_peak[..., None]), 0.0)
    part_total = jnp.sum(weights, axis=3)
    part_mixed = jnp.einsum(
        "rgjt,tgd->rgjd",
        weights.astype(jnp.bfloat16),
        projected_value_rows.reshape(row_count, kv_heads, head_dim),
        preferred_element_type=jnp.float32,
    )
    return (part_peak, part_total, part_mixed)


def on_device(
    tokens, new_token_states, w_query, key_matrix, value_matrix, w_out, lengths, block_map
):
    local_rows = tokens.shape[0]
    block_rows = local_rows // 2
    request_count = new_token_states.shape[0]
    head_dim = HEAD_SIZE
    query_width = w_query.shape[1]
    kv_width = key_matrix.shape[1]
    kv_heads = kv_width // head_dim
    query_group_count = query_width // kv_width
    score_scale = 1.0 / math.sqrt(head_dim)
    device = lax.axis_index("ctx")
    request_ends = jnp.cumsum(lengths)
    inputs = jnp.concatenate([tokens, new_token_states], axis=0)
    joined = lax.all_gather(
        jnp.concatenate([w_query, key_matrix, value_matrix, w_out.T], axis=1),
        "ctx",
        axis=0,
        tiled=True,
    )
    qkv_width = query_width + 2 * kv_width
    projected_all = jnp.dot(
        inputs, joined[:, :qkv_width], preferred_element_type=jnp.float32
    ).astype(jnp.bfloat16)
    out_weight = joined[:, qkv_width:].T
    query_all = projected_all[:, :query_width]
    key_all = projected_all[:, query_width : query_width + kv_width]
    value_all = projected_all[:, query_width + kv_width :]
    local_query = query_all[:local_rows]
    local_keys = key_all[:local_rows]
    local_values = value_all[:local_rows]
    dec_query = query_all[local_rows:]
    decode_key_rows = key_all[local_rows:]
    decode_value_rows = value_all[local_rows:]
    token_pos = initial_positions(block_map, device * local_rows, local_rows, block_rows)
    token_request = request_index(token_pos, request_ends)
    query_heads = local_query.reshape(local_rows, kv_heads, query_group_count, head_dim)

    def attend(running, shard_pieces, first_row):
        peak_run, total_run, mixed_run = running
        key_piece, value_piece = shard_pieces
        row_count = key_piece.shape[0]
        key_pos = initial_positions(block_map, first_row, row_count, block_rows)
        key_request = request_index(key_pos, request_ends)
        allowed = (key_request[None, :] == token_request[:, None]) & (
            key_pos[None, :] <= token_pos[:, None]
        )
        scores = (
            jnp.einsum(
                "tgjd,kgd->gjtk",
                query_heads,
                key_piece.reshape(row_count, kv_heads, head_dim),
                preferred_element_type=jnp.float32,
            )
            * score_scale
        )
        scores = jnp.where(allowed, scores, floor_value)
        peak_new = jnp.maximum(peak_run, jnp.max(scores, axis=3))
        weights = jnp.where(allowed, jnp.exp(scores - peak_new[..., None]), 0.0)
        rescale = jnp.exp(peak_run - peak_new)
        total_new = total_run * rescale + jnp.sum(weights, axis=3)
        mixed_new = mixed_run * rescale[..., None] + jnp.einsum(
            "gjtk,kgd->gjtd",
            weights.astype(jnp.bfloat16),
            value_piece.reshape(row_count, kv_heads, head_dim),
            preferred_element_type=jnp.float32,
        )
        return (peak_new, total_new, mixed_new)

    start_state = (
        jnp.full((kv_heads, query_group_count, local_rows), floor_value, jnp.float32),
        jnp.zeros((kv_heads, query_group_count, local_rows), jnp.float32),
        jnp.zeros((kv_heads, query_group_count, local_rows, head_dim), jnp.float32),
    )
    dec_heads = dec_query.reshape(request_count, kv_heads, query_group_count, head_dim)
    request_ids = jnp.arange(request_count, dtype=jnp.int32)
    cache_both = lax.all_gather(
        jnp.concatenate([local_keys, local_values], axis=1), "ctx", axis=0, tiled=True
    )
    cache_keys = cache_both[:, :kv_width]
    cache_values = cache_both[:, kv_width:]
    total_rows = cache_keys.shape[0]
    shard_count = total_rows // local_rows
    limit = max(1, 1024 // local_rows)
    step_rows = local_rows * math.gcd(shard_count, 1 << limit.bit_length() - 1)

    def key_step(running, step_index):
        first_row = step_index * step_rows
        pieces = (
            lax.dynamic_slice_in_dim(cache_keys, first_row, step_rows, 0),
            lax.dynamic_slice_in_dim(cache_values, first_row, step_rows, 0),
        )
        return (attend(running, pieces, first_row), None)

    final_state, unused = lax.scan(
        key_step, start_state, jnp.arange(total_rows // step_rows, dtype=jnp.int32)
    )
    peak_run, total_run, mixed_run = final_state
    cache_pos = (
        block_map[:, None] * block_rows + jnp.arange(block_rows, dtype=jnp.int32)[None, :]
    ).reshape(total_rows)
    cache_request = request_index(cache_pos, request_ends)
    owned = (cache_request[None, :] == request_ids[:, None])[:, None, None, :]
    cache_peak, cache_total, cache_mixed = softmax_parts(
        dec_heads, cache_keys, cache_values, owned, kv_heads, head_dim, score_scale
    )
    attended = (
        (mixed_run / total_run[..., None]).transpose(2, 0, 1, 3).reshape(local_rows, query_width)
    )
    attended = attended.astype(jnp.bfloat16)
    own_keys = decode_key_rows.reshape(request_count, kv_heads, 1, head_dim).astype(jnp.float32)
    own_values = decode_value_rows.reshape(request_count, kv_heads, 1, head_dim).astype(jnp.float32)
    self_scores = jnp.sum(dec_heads.astype(jnp.float32) * own_keys, axis=3) * score_scale
    peak_all = jnp.maximum(cache_peak, self_scores)
    rescale = jnp.exp(cache_peak - peak_all)
    self_weights = jnp.exp(self_scores - peak_all)
    dec_total = cache_total * rescale + self_weights
    dec_mixed = (
        cache_mixed * rescale[..., None] + round_weights(self_weights)[..., None] * own_values
    )
    dec_attn = (
        (dec_mixed / dec_total[..., None]).reshape(request_count, query_width).astype(jnp.bfloat16)
    )
    attended_all = jnp.concatenate([attended, dec_attn], axis=0)
    projected = jnp.dot(attended_all, out_weight, preferred_element_type=jnp.float32)
    summed_rows = lax.psum_scatter(
        projected.astype(jnp.bfloat16), "tp", scatter_dimension=1, tiled=True
    ).astype(jnp.float32)
    summed_rows = summed_rows.astype(jnp.bfloat16)
    return (summed_rows[:local_rows], summed_rows[local_rows:])


def solution(mesh):
    return jax.shard_map(
        on_device,
        mesh=mesh,
        in_specs=(
            P("ctx", None),
            P(),
            P("ctx", "tp"),
            P("ctx", "tp"),
            P("ctx", "tp"),
            P("tp", "ctx"),
            P(),
            P(),
        ),
        out_specs=(P("ctx", "tp"), P(None, "tp")),
        check_vma=False,
    )
```

profile of v0, /device:TPU:17, one launch (start us, length us, event | category | flops | bytes accessed | tf_op | source)
XLA Modules:
  0.0 756.4 jit_solution(10160451759107932689)
XLA Ops:
  7.2 1.5 pad_maximum_fusion
  8.8 288.3 %all-gather.3.cloned.1.call-done = bf16[4096,768]{1,0:T(8,128)(2,1)} async-done(((bf16[64,768]{1,0:T(8,128)(2,1)}), bf16[4096,768]{1,0:T(8,128)(2,1)}) %all-gather.3.cloned.1.call-update) | async-done | bytes 6291472 | tf_op jit(solution)/shard_map/all_gather | solution.py:72
  297.0 3.3 fusion.33
  300.3 0.6 fusion.85
  301.2 0.7 broadcast_multiply_fusion
  302.1 0.8 select_reduce_fusion.1
  303.5 1.3 convert_reduce_fusion.2
  305.2 308.1 %all-gather.5.cloned.1.call-done = bf16[8192,256]{1,0:T(8,128)(2,1)} async-done(((bf16[128,256]{1,0:T(8,128)(2,1)}), bf16[8192,256]{1,0:T(8,128)(2,1)}) %all-gather.5.cloned.1.call-update) | async-done | bytes 4194320 | tf_op jit(solution)/shard_map/all_gather | solution.py:134
  613.3 2.3 fusion.86
  615.9 2.0 fusion.57
  618.2 3.8 fusion.84
  622.0 43.6 %while.17 = (s32[]{:T(128)}, f32[1,2,128]{2,1,0:T(2,128)S(1)}, f32[1,2,128]{2,1,0:T(2,128)S(1)}, f32[1,2,128,128]{3,2,1,0:T(8,128)S(1)}, s32[8]{0:T(128)S(1)}, /...) while((s32[]{:T(128)}, f32[1,2,128]{2,1,0:T(2,128)S(1)}, ...), condition=%wide.region_8.9_spmd.clone, body=%wide.region_3.8_spmd.clone.sunk | while | flops 137504256 | bytes 4577331 | solution.py:152
  622.0 0.6 dynamic_slice.37
  623.2 1.0 select_reduce_fusion.3
  624.3 1.0 compare_and_fusion.2
  625.7 1.4 fusion.100
  627.4 0.6 dynamic_slice.37
  628.7 1.0 select_reduce_fusion.3
  629.8 1.0 compare_and_fusion.2
  631.2 1.4 fusion.100
  632.9 0.6 dynamic_slice.37
  634.1 1.0 select_reduce_fusion.3
  635.2 1.0 compare_and_fusion.2
  636.7 1.4 fusion.100
  638.3 0.6 dynamic_slice.37
  639.6 1.0 select_reduce_fusion.3
  640.7 1.0 compare_and_fusion.2
  642.1 1.4 fusion.100
  643.8 0.6 dynamic_slice.37
  645.0 1.0 select_reduce_fusion.3
  646.2 1.0 compare_and_fusion.2
  647.6 1.4 fusion.100
  649.2 0.6 dynamic_slice.37
  650.5 1.0 select_reduce_fusion.3
  651.6 1.0 compare_and_fusion.2
  653.0 1.4 fusion.100
  654.7 0.6 dynamic_slice.37
  656.0 1.0 select_reduce_fusion.3
  657.1 1.0 compare_and_fusion.2
  658.5 1.4 fusion.100
  660.2 0.6 dynamic_slice.37
  661.4 1.0 select_reduce_fusion.3
  662.5 1.0 compare_and_fusion.2
  663.9 1.4 fusion.100
  665.7 3.5 convolution_convert_fusion
  669.2 77.8 %reduce-scatter.2.cloned.1.call-done = bf16[132,512]{1,0:T(8,128)(2,1)} async-done(((bf16[132,4096]{1,0:T(8,128)(2,1)}), bf16[132,512]{1,0:T(8,128)(2,1)}) %reduce-scatter.2.cloned.1.call-update) | async-done | bytes 135184 | tf_op jit(solution)/shard_map/reduce_scatter | solution.py:183
  747.0 1.6 slice.60
  748.6 1.3 slice.61
  (129 shorter events, 7.8 us)
Async XLA Ops:
  7.2 289.9 %all-gather.3.cloned.1.call-start = ((), (), s32[]{:S(2)}) async-start(), calls=%async_computation.1 | async-start | bytes 6389760 | tf_op jit(solution)/shard_map/all_gather | solution.py:72
  8.7 292.4 %copy-start = (s32[4]{0:T(128)S(1)}, s32[4]{0:T(128)}, u32[]{:S(2)}) copy-start(s32[4]{0:T(128)} %param.16) | copy-start | bytes 52
  8.7 604.6 %all-gather.5.cloned.1.call-start = ((), (), s32[]{:S(2)}) async-start(), calls=%async_computation.2 | async-start | bytes 4259840 | tf_op jit(solution)/shard_map/all_gather | solution.py:134
  301.0 446.0 %reduce-scatter.2.cloned.1.call-start = ((), (), s32[]{:S(2)}) async-start(), calls=%async_computation.3 | async-start | bytes 1253376 | tf_op jit(solution)/shard_map/reduce_scatter | solution.py:183
  622.0 3.4 copy-start.1
  625.7 1.6 copy-start.2
  627.4 3.4 copy-start.1
  631.2 1.6 copy-start.2
  632.9 3.4 copy-start.1
  636.6 1.6 copy-start.2
  638.3 3.4 copy-start.1
  642.1 1.6 copy-start.2
  643.8 3.4 copy-start.1
  647.6 1.6 copy-start.2
  649.2 3.4 copy-start.1
  653.0 1.6 copy-start.2
  654.7 3.4 copy-start.1
  658.5 1.6 copy-start.2
  660.1 3.4 copy-start.1
  663.9 1.6 copy-start.2
Sparse Core Ops, SparseCore 0:
  10.7 286.3 all-gather.2
  301.1 312.1 all-gather.4
  669.3 77.5 reduce-scatter.1
where the time goes:
time: 757 us; the launch traced here: 756 us
  waiting for transfers between devices  674 us (89%)
  matrix products  24.9 us (3%)
  other arithmetic  24.7 us (3%)
  between operations  13.9 us (2%)
  local copies, waits for them, and re-layouts  12.5 us (2%)
    all_gather x1, waiting for transfers between devices, on_device(): lax.all_gather(jnp.concatenate([local_keys, local_values], axis=1), 'ctx'...  308 us
    all_gather x1, waiting for transfers between devices, on_device(): lax.all_gather(jnp.concatenate([w_query, key_matrix, value_matrix, w_out....  288 us
    reduce_scatter x1, waiting for transfers between devices, on_device(): lax.psum_scatter(projected.astype(jnp.bfloat16), 'tp', scatter_dimension=...  77.8 us
  transfers between devices with their start and end apart: 3, of which 3 were waited for; matrix products, arithmetic and copies ran while one was open for 1% of the time, Pallas kernels for 0%

commit v1 on v0

--- a/solution.py
+++ b/solution.py
@@ -69,11 +69,17 @@
     device = lax.axis_index("ctx")
     request_ends = jnp.cumsum(lengths)
     inputs = jnp.concatenate([tokens, new_token_states], axis=0)
-    joined = lax.all_gather(
-        jnp.concatenate([w_query, key_matrix, value_matrix, w_out.T], axis=1),
-        "ctx",
+    joined = jnp.concatenate(
+        lax.all_to_all(
+            jnp.stack(
+                [jnp.concatenate([w_query, key_matrix, value_matrix, w_out.T], axis=1)]
+                * lax.axis_size("ctx")
+            ),
+            "ctx",
+            0,
+            0,
+        ),
         axis=0,
-        tiled=True,
     )
     qkv_width = query_width + 2 * kv_width
     projected_all = jnp.dot(

time: 757 us -> 584 us (0.77)
  waiting for transfers between devices: 674 us -> 348 us
  blocking collectives: 0 us -> 153 us
    all_gather x1 -> x0, waiting for transfers between devices: 288 us -> none  [on_device(): lax.all_gather(jnp.concatenate([w_query, key_matrix, value_matrix, w_out....]
    all_to_all x0 -> x1, blocking collectives: none -> 153 us  [on_device(): lax.all_to_all(jnp.stack([jnp.concatenate([w_query, key_matrix, value_mat...]
    all_gather x1, waiting for transfers between devices: 308 us -> 270 us  [on_device(): lax.all_gather(jnp.concatenate([local_keys, local_values], axis=1), 'ctx'...]
  transfers between devices with their start and end apart: 3 -> 2, of which waited for: 3 -> 2; matrix products, arithmetic and copies ran while one was open for 1% -> 1% of each run, Pallas kernels for 0% -> 0%
where the time goes in v1:
time: 584 us; the launch traced here: 583 us
  waiting for transfers between devices  348 us (60%)
  blocking collectives  153 us (26%)
  other arithmetic  24.1 us (4%)
  matrix products  22.4 us (4%)
  local copies, waits for them, and re-layouts  15.2 us (3%)
  between operations  14.2 us (2%)
  loops' own time  6.07 us (1%)
    all_gather x1, waiting for transfers between devices, on_device(): lax.all_gather(jnp.concatenate([local_keys, local_values], axis=1), 'ctx'...  270 us
    all_to_all x1, blocking collectives, on_device(): lax.all_to_all(jnp.stack([jnp.concatenate([w_query, key_matrix, value_mat...  153 us
    reduce_scatter x1, waiting for transfers between devices, on_device(): lax.psum_scatter(projected.astype(jnp.bfloat16), 'tp', scatter_dimension=...  77.9 us
  transfers between devices with their start and end apart: 2, of which 2 were waited for; matrix products, arithmetic and copies ran while one was open for 1% of the time, Pallas kernels for 0%

profile of v1, /device:TPU:17, one launch (start us, length us, event | category | flops | bytes accessed | tf_op | source)
XLA Modules:
  0.0 583.4 jit_solution(3903232740004640046)
XLA Ops:
  7.2 0.8 pad_maximum_fusion
  8.0 0.8 stack.2
  8.8 153.5 %all_to_all.5 = bf16[64,64,768]{2,1,0:T(8,128)(2,1)S(1)} all-to-all(bf16[64,64,768]{2,1,0:T(8,128)(2,1)S(1)} %stack.2), channel_id=1, replica_groups=mesh['ctx'=64,'tp'=8] {'ctx'}, dimensions={0} | all-to-all | bytes 12582912 | tf_op jit(solution)/shard_map/all_to_all | solution.py:73
  162.3 0.8 fusion.33
  163.1 1.9 copy-done
  164.9 0.6 fusion.85
  165.9 0.7 broadcast_multiply_fusion
  166.7 0.8 select_reduce_fusion.1
  168.1 1.3 convert_reduce_fusion.2
  169.9 270.0 %all-gather.2.cloned.1.call-done = bf16[8192,256]{1,0:T(8,128)(2,1)} async-done(((bf16[128,256]{1,0:T(8,128)(2,1)}), bf16[8192,256]{1,0:T(8,128)(2,1)}) %all-gather.2.cloned.1.call-update) | async-done | bytes 4194320 | tf_op jit(solution)/shard_map/all_gather | solution.py:140
  439.8 2.3 fusion.86
  442.5 2.0 fusion.57
  444.7 3.8 fusion.84
  448.5 43.6 %while.17 = (s32[]{:T(128)}, f32[1,2,128]{2,1,0:T(2,128)S(1)}, f32[1,2,128]{2,1,0:T(2,128)S(1)}, f32[1,2,128,128]{3,2,1,0:T(8,128)S(1)}, s32[8]{0:T(128)S(1)}, /...) while((s32[]{:T(128)}, f32[1,2,128]{2,1,0:T(2,128)S(1)}, ...), condition=%wide.region_8.9_spmd.clone, body=%wide.region_3.8_spmd.clone.sunk | while | flops 137504256 | bytes 4577331 | solution.py:158
  449.8 1.0 select_reduce_fusion.3
  450.9 1.0 compare_and_fusion.2
  452.3 1.4 fusion.100
  454.0 0.6 dynamic_slice.37
  455.2 1.0 select_reduce_fusion.3
  456.3 1.0 compare_and_fusion.2
  457.8 1.4 fusion.100
  459.4 0.6 dynamic_slice.37
  460.7 1.0 select_reduce_fusion.3
  461.8 1.0 compare_and_fusion.2
  463.2 1.4 fusion.100
  464.9 0.6 dynamic_slice.37
  466.1 1.0 select_reduce_fusion.3
  467.3 1.0 compare_and_fusion.2
  468.7 1.4 fusion.100
  470.3 0.6 dynamic_slice.37
  471.6 1.0 select_reduce_fusion.3
  472.7 1.0 compare_and_fusion.2
  474.1 1.4 fusion.100
  477.1 1.0 select_reduce_fusion.3
  478.2 1.0 compare_and_fusion.2
  479.6 1.4 fusion.100
  481.3 0.6 dynamic_slice.37
  482.5 1.0 select_reduce_fusion.3
  483.6 1.0 compare_and_fusion.2
  485.0 1.4 fusion.100
  486.7 0.6 dynamic_slice.37
  488.0 1.0 select_reduce_fusion.3
  489.1 1.0 compare_and_fusion.2
  490.5 1.4 fusion.100
  492.3 3.5 convolution_convert_fusion
  495.8 77.9 %reduce-scatter.2.cloned.1.call-done = bf16[132,512]{1,0:T(8,128)(2,1)} async-done(((bf16[132,4096]{1,0:T(8,128)(2,1)}), bf16[132,512]{1,0:T(8,128)(2,1)}) %reduce-scatter.2.cloned.1.call-update) | async-done | bytes 135184 | tf_op jit(solution)/shard_map/reduce_scatter | solution.py:189
  573.7 1.6 slice.60
  575.3 1.3 slice.61
  (134 shorter events, 8.9 us)
Async XLA Ops:
  7.2 432.7 %all-gather.2.cloned.1.call-start = ((), (), s32[]{:S(2)}) async-start(), calls=%async_computation.2 | async-start | bytes 4259840 | tf_op jit(solution)/shard_map/all_gather | solution.py:140
  8.8 153.5 %copy-start.1 = (bf16[128,4096]{1,0:T(8,128)(2,1)S(1)}, bf16[128,4096]{1,0:T(8,128)(2,1)}, u32[]{:S(2)}) copy-start(bf16[128,4096]{1,0:T(8,128)(2,1)} %param.10) | copy-start | bytes 3145732
  8.8 153.5 %copy-start.2 = (bf16[4,4096]{1,0:T(4,128)(2,1)S(1)}, bf16[4,4096]{1,0:T(4,128)(2,1)}, u32[]{:S(2)}) copy-start(bf16[4,4096]{1,0:T(4,128)(2,1)} %param.11) | copy-start | bytes 98308
  162.3 2.7 copy-start
  162.3 3.4 copy-start.3
  165.6 408.1 %reduce-scatter.2.cloned.1.call-start = ((), (), s32[]{:S(2)}) async-start(), calls=%async_computation.3 | async-start | bytes 1253376 | tf_op jit(solution)/shard_map/reduce_scatter | solution.py:189
  448.5 3.4 copy-start.4
  452.3 1.6 copy-start.5
  454.0 3.4 copy-start.4
  457.7 1.6 copy-start.5
  459.4 3.4 copy-start.4
  463.2 1.6 copy-start.5
  464.9 3.4 copy-start.4
  468.7 1.6 copy-start.5
  470.3 3.4 copy-start.4
  474.1 1.6 copy-start.5
  475.8 3.4 copy-start.4
  479.6 1.6 copy-start.5
  481.2 3.4 copy-start.4
  485.0 1.6 copy-start.5
  486.7 3.4 copy-start.4
  490.5 1.6 copy-start.5
Sparse Core Ops, SparseCore 0:
  165.7 274.0 all-gather.1
  495.9 77.7 reduce-scatter.1
